TPU v7x, 32 devices: a whole 2x2x4 slice. The times are simulated.
32 devices in a mesh: row: 8 (over z, y), col: 4 (over x, core).
Axes of the slice: x: 2, y: 2, z: 4, core: 2. Of those that a mesh axis runs over, the one named last changes fastest.
Arguments:
- momentum: float32 [8192, 16384], P('row', 'col'), may hold values from -6 to 6
- grads: bfloat16 [2, 8192, 16384], P(None, 'row', 'col'), may hold values from -400 to 400
- basis: float32 [16384, 256], P('col'), may hold values from -0.046875 to 0.046875
Outputs:
- change: bfloat16 [8192, 16384], P('row', 'col')
- state: float32 [8192, 16384], P('row', 'col')
All inputs are finite; a program needn't handle non-finite values.
Results may differ from a plain program's by a relative error of at most 0.0035.
Values sent between devices are 32-bit elements; how exact they have to be, the bound alone decides.
A program may use at most 192 MiB of HBM per device.

v0:
```python
import jax
import jax.numpy as jnp
from jax import lax
from jax.sharding import PartitionSpec as P

ROWS = 8192
COLS = 16384
RANK = 256
STEPS = 2
keep_rate = 0.95
norm_eps = 1e-06


def column_squares(matrix):
    return jnp.sum(matrix * matrix, axis=0)


def shards(momentum, grads, basis):
    high = lax.Precision.HIGHEST
    factor = (ROWS * COLS / RANK) ** 0.5
    state = momentum
    right = basis
    change = jnp.zeros(momentum.shape, jnp.float32)
    for step in range(STEPS):
        buffer = state + grads[step].astype(jnp.float32)
        partial_value = jnp.dot(buffer, right, precision=high, preferred_element_type=jnp.float32)
        projected = lax.psum(partial_value, "col")
        gram = lax.psum(
            jnp.dot(projected.T, projected, precision=high, preferred_element_type=jnp.float32),
            "row",
        )
        lower = jnp.linalg.cholesky(gram)
        ortho = jax.scipy.linalg.solve_triangular(lower, projected.T, lower=True).T
        local_right = lax.dot_general(
            buffer,
            ortho,
            (((0,), (0,)), ((), ())),
            precision=high,
            preferred_element_type=jnp.float32,
        )
        raw = lax.psum(local_right, "row")
        squares = lax.psum(column_squares(raw), "col")
        right = raw * lax.rsqrt(squares + norm_eps)
        state = buffer - (1.0 - keep_rate) * jnp.dot(
            ortho, raw.T, precision=high, preferred_element_type=jnp.float32
        )
        change = change + factor * jnp.dot(
            ortho, right.T, precision=high, preferred_element_type=jnp.float32
        )
    return (change.astype(jnp.bfloat16), state)


def solution(mesh):
    return jax.shard_map(
        shards,
        mesh=mesh,
        in_specs=(P("row", "col"), P(None, "row", "col"), P("col", None)),
        out_specs=(P("row", "col"), P("row", "col")),
        check_vma=False,
    )
```

profile of v0, /device:TPU:0, one launch (start us, length us, event | category | flops | bytes accessed | tf_op | source)
XLA Modules:
  0.0 904.7 jit_solution(4281090039093472297)
XLA Ops:
  7.2 20.3 %fusion.1 = f32[1024,256]{1,0:T(8,128)} fusion(f32[4096,256]{1,0:T(8,128)} %param.8, f32[1024,4096]{1,0:T(8,128)} %param.6, bf16[2,1024,4096]{2,1,0:T(8,128)(2,1)} %param.7), kind=kOutput, calls=%fused_computation.9 | convolution fusion | flops 12893290496 | bytes 30408704 | tf_op jit(solution)/shard_map/dot_general | solution.py:26
  27.6 39.1 %all-reduce.8.cloned.1.call-done = f32[1024,256]{1,0:T(8,128)} async-done(((f32[1024,256]{1,0:T(8,128)}), f32[1024,256]{1,0:T(8,128)}) %all-reduce.8.cloned.1.call-update) | async-done | bytes 1048592 | tf_op jit(solution)/shard_map/psum | solution.py:27
  66.7 4.1 fusion.35
  71.0 71.4 %all-reduce.10.cloned.1.call-done = f32[256,256]{0,1:T(8,128)} async-done(((f32[256,256]{0,1:T(8,128)}), f32[256,256]{0,1:T(8,128)}) %all-reduce.10.cloned.1.call-update) | async-done | bytes 262160 | tf_op jit(solution)/shard_map/psum | solution.py:28
  144.5 11.7 %cholesky.130 = f32[128,128]{1,0:T(8,128)S(1)} custom-call(f32[128,128]{1,0:T(8,128)S(1)} %cholesky.194), custom_call_target="Cholesky" | custom-call | tf_op jit(solution)/shard_map/jit(cholesky)/cholesky | solution.py:32
  156.3 9.8 %custom-call.13 = f32[1,128,128]{1,2,0:T(8,128)S(1)} custom-call(f32[1,128,128]{2,1,0:T(8,128)S(1)} %get-tuple-element.47), custom_call_target="InvertDiagBlocksLowerTriangular" | custom-call | tf_op jit(solution)/shard_map/jit(cholesky)/cholesky | solution.py:32
  166.6 11.7 %cholesky.147 = f32[128,128]{1,0:T(8,128)S(1)} custom-call(f32[128,128]{1,0:T(8,128)S(1)} %convolution_subtract_fusion.3), custom_call_target="Cholesky" | custom-call | tf_op jit(solution)/shard_map/jit(cholesky)/cholesky | solution.py:32
  180.5 4.1 while.4
  184.6 19.7 %custom-call.14 = f32[2,128,128]{1,2,0:T(8,128)S(1)} custom-call(f32[2,128,128]{2,1,0:T(8,128)S(1)} %get-tuple-element.18), custom_call_target="InvertDiagBlocksLowerTriangular" | custom-call | tf_op jit(solution)/shard_map/jit(_solve_triangular)/triangular_solve | solution.py:33
  206.0 2.0 convolution_subtract_fusion.1
  208.7 32.9 %fusion = f32[4096,256]{1,0:T(8,128)} fusion(f32[1024,4096]{1,0:T(8,128)} %param.6, bf16[2,1024,4096]{2,1,0:T(8,128)(2,1)} %param.7, f32[128,1024]{1,0:T(8,128)S(1)} %fusion.22, f32[128,1024]{1,0:T(8,128)S(1)} %fusion.13), kind=kOutput, calls=%fused_computation.8 | convolution fusion | flops 12893552640 | bytes 30408704 | tf_op jit(solution)/shard_map/dot_general | solution.py:34
  241.7 155.7 %all-reduce.12.cloned.1.call-done = f32[4096,256]{1,0:T(8,128)} async-done(((f32[4096,256]{1,0:T(8,128)}), f32[4096,256]{1,0:T(8,128)}) %all-reduce.12.cloned.1.call-update) | async-done | bytes 4194320 | tf_op jit(solution)/shard_map/psum | solution.py:41
  397.4 2.7 multiply_reduce_fusion.1
  400.1 6.4 psum.59
  406.5 36.7 %convert_add_fusion = f32[1024,4096]{1,0:T(8,128)} fusion(f32[4096,256]{1,0:T(8,128)} %all-reduce.12.cloned.1.call-done, bf16[2,1024,4096]{2,1,0:T(8,128)(2,1)} %param.7, f32[1024,4096]{1,0:T(8,128)} %param.6, f32[128,1024]{1,0:T(8,128)S(1)} %fusion.22, f32[128,1024]{1,0:T(8,128)S(1)} %fusion.13), kind=kOutput, calls=%fused_computation.4 | convolution fusion | flops 12910329856 | bytes 55574528 | tf_op jit(solution)/shard_map/dot_general | solution.py:44
  443.3 17.2 %fusion.3 = f32[1024,256]{1,0:T(8,128)} fusion(f32[1024,4096]{1,0:T(8,128)} %convert_add_fusion, f32[4096,256]{1,0:T(8,128)} %all-reduce.12.cloned.1.call-done, f32[256]{0:T(256)S(1)} %add_rsqrt_fusion.1), kind=kOutput, calls=%fused_computation.13 | convolution fusion | flops 12885950464 | bytes 22021120 | tf_op jit(solution)/shard_map/dot_general | solution.py:26
  460.8 34.7 %all-reduce.14.cloned.1.call-done = f32[1024,256]{1,0:T(8,128)} async-done(((f32[1024,256]{1,0:T(8,128)}), f32[1024,256]{1,0:T(8,128)}) %all-reduce.14.cloned.1.call-update) | async-done | bytes 1048592 | tf_op jit(solution)/shard_map/psum | solution.py:27
  495.5 4.1 fusion.36
  499.6 71.6 %all-reduce.16.cloned.1.call-done = f32[256,256]{0,1:T(8,128)} async-done(((f32[256,256]{0,1:T(8,128)}), f32[256,256]{0,1:T(8,128)}) %all-reduce.16.cloned.1.call-update) | async-done | bytes 262160 | tf_op jit(solution)/shard_map/psum | solution.py:28
  573.3 11.7 %cholesky.164 = f32[128,128]{1,0:T(8,128)S(1)} custom-call(f32[128,128]{1,0:T(8,128)S(1)} %cholesky.197), custom_call_target="Cholesky" | custom-call | tf_op jit(solution)/shard_map/jit(cholesky)/cholesky | solution.py:32
  585.7 9.8 %custom-call.15 = f32[1,128,128]{1,2,0:T(8,128)S(1)} custom-call(f32[1,128,128]{2,1,0:T(8,128)S(1)} %get-tuple-element.43), custom_call_target="InvertDiagBlocksLowerTriangular" | custom-call | tf_op jit(solution)/shard_map/jit(cholesky)/cholesky | solution.py:32
  596.0 11.7 %cholesky.181 = f32[128,128]{1,0:T(8,128)S(1)} custom-call(f32[128,128]{1,0:T(8,128)S(1)} %convolution_subtract_fusion.2), custom_call_target="Cholesky" | custom-call | tf_op jit(solution)/shard_map/jit(cholesky)/cholesky | solution.py:32
  609.9 4.5 while.5
  614.4 19.7 %custom-call.16 = f32[2,128,128]{1,2,0:T(8,128)S(1)} custom-call(f32[2,128,128]{2,1,0:T(8,128)S(1)} %get-tuple-element.19), custom_call_target="InvertDiagBlocksLowerTriangular" | custom-call | tf_op jit(solution)/shard_map/jit(_solve_triangular)/triangular_solve | solution.py:33
  635.8 2.0 convolution_subtract_fusion
  638.5 29.9 %fusion.10 = f32[4096,256]{1,0:T(8,128)} fusion(f32[1024,4096]{1,0:T(8,128)} %convert_add_fusion, f32[128,1024]{1,0:T(8,128)S(1)} %fusion.18, f32[128,1024]{1,0:T(8,128)S(1)} %fusion.11), kind=kOutput, calls=%fused_computation.26 | convolution fusion | flops 12885164032 | bytes 22020096 | tf_op jit(solution)/shard_map/dot_general | solution.py:34
  668.4 30.2 %fusion.5 = f32[1024,4096]{1,0:T(8,128)} fusion(f32[4096,256]{1,0:T(8,128)} %all-reduce.12.cloned.1.call-done, f32[256]{0:T(256)S(1)} %add_rsqrt_fusion.1, f32[128,1024]{1,0:T(8,128)S(1)} %fusion.22, f32[128,1024]{1,0:T(8,128)S(1)} %fusion.13), kind=kOutput, calls=%fused_computation.15 | convolution fusion | flops 12886212608 | bytes 22021120 | tf_op jit(solution)/shard_map/dot_general | solution.py:47
  698.5 125.6 %all-reduce.18.cloned.1.call-done = f32[4096,256]{1,0:T(8,128)} async-done(((f32[4096,256]{1,0:T(8,128)}), f32[4096,256]{1,0:T(8,128)}) %all-reduce.18.cloned.1.call-update) | async-done | bytes 4194320 | tf_op jit(solution)/shard_map/psum | solution.py:41
  824.1 2.7 multiply_reduce_fusion
  826.9 6.6 psum.63
  833.5 33.4 %multiply_subtract_fusion = f32[1024,4096]{1,0:T(8,128)} fusion(f32[1024,4096]{1,0:T(8,128)} %convert_add_fusion, f32[4096,256]{1,0:T(8,128)} %all-reduce.18.cloned.1.call-done, f32[128,1024]{1,0:T(8,128)S(1)} %fusion.18, f32[128,1024]{1,0:T(8,128)S(1)} %fusion.11), kind=kOutput, calls=%fused_computation.7 | convolution fusion | flops 12893552640 | bytes 38797312 | tf_op jit(solution)/shard_map/dot_general | solution.py:44
  866.9 30.6 %multiply_convert_fusion = bf16[1024,4096]{1,0:T(8,128)(2,1)} fusion(f32[1024,4096]{1,0:T(8,128)} %fusion.5, f32[4096,256]{1,0:T(8,128)S(1)} %copy-done, f32[256]{0:T(256)S(1)} %add_rsqrt_fusion, f32[128,1024]{1,0:T(8,128)S(1)} %fusion.18, f32[128,1024]{1,0:T(8,128)S(1)} %fusion.11), kind=kOutput, calls=%fused_computation.6 | convolution fusion | flops 12898795520 | bytes 30409728 | tf_op jit(solution)/shard_map/dot_general | solution.py:47
  (57 shorter events, 21.0 us)
Async XLA Ops:
  7.2 59.5 %all-reduce.8.cloned.1.call-start = ((), (), s32[]{:S(2)}) async-start(), calls=%async_computation | async-start | bytes 2097152 | tf_op jit(solution)/shard_map/psum | solution.py:27
  27.5 114.9 %all-reduce.10.cloned.1.call-start = ((), (), s32[]{:S(2)}) async-start(), calls=%async_computation.1 | async-start | bytes 524288 | tf_op jit(solution)/shard_map/psum | solution.py:28
  70.8 326.6 %all-reduce.12.cloned.1.call-start = ((), (), s32[]{:S(2)}) async-start(), calls=%async_computation.2 | async-start | bytes 8388608 | tf_op jit(solution)/shard_map/psum | solution.py:41
  241.6 253.9 %all-reduce.14.cloned.1.call-start = ((), (), s32[]{:S(2)}) async-start(), calls=%async_computation.3 | async-start | bytes 2097152 | tf_op jit(solution)/shard_map/psum | solution.py:27
  460.5 110.7 %all-reduce.16.cloned.1.call-start = ((), (), s32[]{:S(2)}) async-start(), calls=%async_computation.4 | async-start | bytes 524288 | tf_op jit(solution)/shard_map/psum | solution.py:28
  499.6 324.5 %all-reduce.18.cloned.1.call-start = ((), (), s32[]{:S(2)}) async-start(), calls=%async_computation.5 | async-start | bytes 8388608 | tf_op jit(solution)/shard_map/psum | solution.py:41
  833.5 33.5 %copy-start = (f32[4096,256]{1,0:T(8,128)S(1)}, f32[4096,256]{1,0:T(8,128)}, u32[]{:S(2)}) copy-start(f32[4096,256]{1,0:T(8,128)} %all-reduce.18.cloned.1.call-done) | copy-start | bytes 12582916
Sparse Core Ops, SparseCore 0:
  27.7 39.0 all-reduce.7
  70.9 71.4 all-reduce.9
  241.8 155.5 all-reduce.11
  460.7 34.8 all-reduce.13
  499.7 71.4 all-reduce.15
  668.5 155.5 all-reduce.17
where the time goes:
time: 911 us; the launch traced here: 905 us
  waiting for transfers between devices  498 us (55%)
  matrix products  249 us (27%)
  other arithmetic  116 us (13%)
  between operations  17.3 us (2%)
  blocking collectives  13 us (1%)
  local copies, waits for them, and re-layouts  10.4 us (1%)
    psum x2, waiting for transfers between devices, shards(): raw = lax.psum(local_right, 'row')  281 us
    psum x2, waiting for transfers between devices, shards(): lax.psum(jnp.dot(projected.T, projected, precision=high, preferred_elemen...  143 us
    psum x2, waiting for transfers between devices, shards(): projected = lax.psum(partial_value, 'col')  73.8 us
    dot_general x2, matrix products, shards(): jnp.dot(ortho, raw.T, precision=high, preferred_element_type=jnp.float32)  70.2 us
    another operation x13, other arithmetic, shards(): lower = jnp.linalg.cholesky(gram)  68.7 us
    dot_general x2, matrix products, shards(): lax.dot_general(buffer, ortho, (((0,), (0,)), ((), ())), precision=high,...  62.8 us
    dot_general x2, matrix products, shards(): jnp.dot(ortho, right.T, precision=high, preferred_element_type=jnp.float32)  60.8 us
    another operation x5, other arithmetic, shards(): ortho = jax.scipy.linalg.solve_triangular(lower, projected.T, lower=True).T  39.4 us
  transfers between devices with their start and end apart: 6, of which 6 were waited for; matrix products, arithmetic and copies ran while one was open for 3% of the time, Pallas kernels for 0%

commit v1 on v0

--- a/solution.py
+++ b/solution.py
@@ -25,9 +25,12 @@
         buffer = state + grads[step].astype(jnp.float32)
         partial_value = jnp.dot(buffer, right, precision=high, preferred_element_type=jnp.float32)
         projected = lax.psum(partial_value, "col")
-        gram = lax.psum(
-            jnp.dot(projected.T, projected, precision=high, preferred_element_type=jnp.float32),
-            "row",
+        gram = jnp.sum(
+            lax.all_gather(
+                jnp.dot(projected.T, projected, precision=high, preferred_element_type=jnp.float32),
+                "row",
+            ),
+            axis=0,
         )
         lower = jnp.linalg.cholesky(gram)
         ortho = jax.scipy.linalg.solve_triangular(lower, projected.T, lower=True).T

time: 911 us -> 865 us (0.950)
  waiting for transfers between devices: 498 us -> 453 us
    psum x2 -> x0, waiting for transfers between devices: 143 us -> none  [shards(): lax.psum(jnp.dot(projected.T, projected, precision=high, preferred_elemen...]
    all_gather x0 -> x2, waiting for transfers between devices: none -> 99.2 us  [shards(): lax.all_gather(jnp.dot(projected.T, projected, precision=high, preferred_...]
  transfers between devices with their start and end apart: 6 -> 6, of which waited for: 6 -> 6; matrix products, arithmetic and copies ran while one was open for 3% -> 4% of each run, Pallas kernels for 0% -> 0%
where the time goes in v1:
time: 865 us; the launch traced here: 859 us
  waiting for transfers between devices  453 us (52%)
  matrix products  249 us (29%)
  other arithmetic  117 us (14%)
  between operations  17.3 us (2%)
  blocking collectives  13 us (2%)
    psum x2, waiting for transfers between devices, shards(): raw = lax.psum(local_right, 'row')  280 us
    all_gather x2, waiting for transfers between devices, shards(): lax.all_gather(jnp.dot(projected.T, projected, precision=high, preferred_...  99.2 us
    psum x2, waiting for transfers between devices, shards(): projected = lax.psum(partial_value, 'col')  73.8 us
    dot_general x2, matrix products, shards(): jnp.dot(ortho, raw.T, precision=high, preferred_element_type=jnp.float32)  70.2 us
    another operation x13, other arithmetic, shards(): lower = jnp.linalg.cholesky(gram)  68.7 us
    dot_general x2, matrix products, shards(): lax.dot_general(buffer, ortho, (((0,), (0,)), ((), ())), precision=high,...  62.8 us
    dot_general x2, matrix products, shards(): jnp.dot(ortho, right.T, precision=high, preferred_element_type=jnp.float32)  60.8 us
    another operation x5, other arithmetic, shards(): ortho = jax.scipy.linalg.solve_triangular(lower, projected.T, lower=True).T  39.4 us
  transfers between devices with their start and end apart: 6, of which 6 were waited for; matrix products, arithmetic and copies ran while one was open for 4% of the time, Pallas kernels for 0%

profile of v1, /device:TPU:0, one launch (start us, length us, event | category | flops | bytes accessed | tf_op | source)
XLA Modules:
  0.0 859.3 jit_solution(12597806348821083547)
XLA Ops:
  7.2 20.3 %fusion.1 = f32[1024,256]{1,0:T(8,128)} fusion(f32[4096,256]{1,0:T(8,128)} %param.8, f32[1024,4096]{1,0:T(8,128)} %param.6, bf16[2,1024,4096]{2,1,0:T(8,128)(2,1)} %param.7), kind=kOutput, calls=%fused_computation.9 | convolution fusion | flops 12893290496 | bytes 30408704 | tf_op jit(solution)/shard_map/dot_general | solution.py:26
  27.6 39.1 %all-reduce.6.cloned.1.call-done = f32[1024,256]{1,0:T(8,128)} async-done(((f32[1024,256]{1,0:T(8,128)}), f32[1024,256]{1,0:T(8,128)}) %all-reduce.6.cloned.1.call-update) | async-done | bytes 1048592 | tf_op jit(solution)/shard_map/psum | solution.py:27
  66.7 4.1 fusion.35
  71.1 49.5 %all-gather.5.cloned.1.call-done = f32[2048,256]{1,0:T(8,128)} async-done(((f32[256,256]{1,0:T(8,128)}), f32[2048,256]{1,0:T(8,128)}) %all-gather.5.cloned.1.call-update) | async-done | bytes 2097168 | tf_op jit(solution)/shard_map/all_gather | solution.py:29
  122.5 11.7 %cholesky.130 = f32[128,128]{1,0:T(8,128)S(1)} custom-call(f32[128,128]{1,0:T(8,128)S(1)} %cholesky.194), custom_call_target="Cholesky" | custom-call | tf_op jit(solution)/shard_map/jit(cholesky)/cholesky | solution.py:35
  134.2 9.8 %custom-call.13 = f32[1,128,128]{1,2,0:T(8,128)S(1)} custom-call(f32[1,128,128]{2,1,0:T(8,128)S(1)} %get-tuple-element.47), custom_call_target="InvertDiagBlocksLowerTriangular" | custom-call | tf_op jit(solution)/shard_map/jit(cholesky)/cholesky | solution.py:35
  144.6 11.7 %cholesky.147 = f32[128,128]{1,0:T(8,128)S(1)} custom-call(f32[128,128]{1,0:T(8,128)S(1)} %convolution_subtract_fusion.3), custom_call_target="Cholesky" | custom-call | tf_op jit(solution)/shard_map/jit(cholesky)/cholesky | solution.py:35
  158.5 4.1 while.4
  162.6 19.7 %custom-call.14 = f32[2,128,128]{1,2,0:T(8,128)S(1)} custom-call(f32[2,128,128]{2,1,0:T(8,128)S(1)} %get-tuple-element.18), custom_call_target="InvertDiagBlocksLowerTriangular" | custom-call | tf_op jit(solution)/shard_map/jit(_solve_triangular)/triangular_solve | solution.py:36
  184.0 2.0 convolution_subtract_fusion.1
  186.7 32.9 %fusion = f32[4096,256]{1,0:T(8,128)} fusion(f32[1024,4096]{1,0:T(8,128)} %param.6, bf16[2,1024,4096]{2,1,0:T(8,128)(2,1)} %param.7, f32[128,1024]{1,0:T(8,128)S(1)} %fusion.22, f32[128,1024]{1,0:T(8,128)S(1)} %fusion.13), kind=kOutput, calls=%fused_computation.8 | convolution fusion | flops 12893552640 | bytes 30408704 | tf_op jit(solution)/shard_map/dot_general | solution.py:37
  219.7 155.0 %all-reduce.8.cloned.1.call-done = f32[4096,256]{1,0:T(8,128)} async-done(((f32[4096,256]{1,0:T(8,128)}), f32[4096,256]{1,0:T(8,128)}) %all-reduce.8.cloned.1.call-update) | async-done | bytes 4194320 | tf_op jit(solution)/shard_map/psum | solution.py:44
  374.7 2.7 multiply_reduce_fusion.1
  377.5 6.4 psum.44
  383.9 36.7 %convert_add_fusion = f32[1024,4096]{1,0:T(8,128)} fusion(f32[4096,256]{1,0:T(8,128)} %all-reduce.8.cloned.1.call-done, bf16[2,1024,4096]{2,1,0:T(8,128)(2,1)} %param.7, f32[1024,4096]{1,0:T(8,128)} %param.6, f32[128,1024]{1,0:T(8,128)S(1)} %fusion.22, f32[128,1024]{1,0:T(8,128)S(1)} %fusion.13), kind=kOutput, calls=%fused_computation.4 | convolution fusion | flops 12910329856 | bytes 55574528 | tf_op jit(solution)/shard_map/dot_general | solution.py:47
  420.6 17.2 %fusion.3 = f32[1024,256]{1,0:T(8,128)} fusion(f32[1024,4096]{1,0:T(8,128)} %convert_add_fusion, f32[4096,256]{1,0:T(8,128)} %all-reduce.8.cloned.1.call-done, f32[256]{0:T(256)S(1)} %add_rsqrt_fusion.1), kind=kOutput, calls=%fused_computation.13 | convolution fusion | flops 12885950464 | bytes 22021120 | tf_op jit(solution)/shard_map/dot_general | solution.py:26
  438.1 34.7 %all-reduce.10.cloned.1.call-done = f32[1024,256]{1,0:T(8,128)} async-done(((f32[1024,256]{1,0:T(8,128)}), f32[1024,256]{1,0:T(8,128)}) %all-reduce.10.cloned.1.call-update) | async-done | bytes 1048592 | tf_op jit(solution)/shard_map/psum | solution.py:27
  472.8 4.1 fusion.36
  476.9 49.7 %all-gather.7.cloned.1.call-done = f32[2048,256]{1,0:T(8,128)} async-done(((f32[256,256]{1,0:T(8,128)}), f32[2048,256]{1,0:T(8,128)}) %all-gather.7.cloned.1.call-update) | async-done | bytes 2097168 | tf_op jit(solution)/shard_map/all_gather | solution.py:29
  528.6 11.7 %cholesky.164 = f32[128,128]{1,0:T(8,128)S(1)} custom-call(f32[128,128]{1,0:T(8,128)S(1)} %cholesky.197), custom_call_target="Cholesky" | custom-call | tf_op jit(solution)/shard_map/jit(cholesky)/cholesky | solution.py:35
  541.0 9.8 %custom-call.15 = f32[1,128,128]{1,2,0:T(8,128)S(1)} custom-call(f32[1,128,128]{2,1,0:T(8,128)S(1)} %get-tuple-element.43), custom_call_target="InvertDiagBlocksLowerTriangular" | custom-call | tf_op jit(solution)/shard_map/jit(cholesky)/cholesky | solution.py:35
  551.3 11.7 %cholesky.181 = f32[128,128]{1,0:T(8,128)S(1)} custom-call(f32[128,128]{1,0:T(8,128)S(1)} %convolution_subtract_fusion.2), custom_call_target="Cholesky" | custom-call | tf_op jit(solution)/shard_map/jit(cholesky)/cholesky | solution.py:35
  565.2 4.5 while.5
  569.7 19.7 %custom-call.16 = f32[2,128,128]{1,2,0:T(8,128)S(1)} custom-call(f32[2,128,128]{2,1,0:T(8,128)S(1)} %get-tuple-element.19), custom_call_target="InvertDiagBlocksLowerTriangular" | custom-call | tf_op jit(solution)/shard_map/jit(_solve_triangular)/triangular_solve | solution.py:36
  591.1 2.0 convolution_subtract_fusion
  593.7 29.9 %fusion.10 = f32[4096,256]{1,0:T(8,128)} fusion(f32[1024,4096]{1,0:T(8,128)} %convert_add_fusion, f32[128,1024]{1,0:T(8,128)S(1)} %fusion.18, f32[128,1024]{1,0:T(8,128)S(1)} %fusion.11), kind=kOutput, calls=%fused_computation.26 | convolution fusion | flops 12885164032 | bytes 22020096 | tf_op jit(solution)/shard_map/dot_general | solution.py:37
  623.6 30.1 %fusion.5 = f32[1024,4096]{1,0:T(8,128)} fusion(f32[4096,256]{1,0:T(8,128)} %all-reduce.8.cloned.1.call-done, f32[256]{0:T(256)S(1)} %add_rsqrt_fusion.1, f32[128,1024]{1,0:T(8,128)S(1)} %fusion.22, f32[128,1024]{1,0:T(8,128)S(1)} %fusion.13), kind=kOutput, calls=%fused_computation.15 | convolution fusion | flops 12886212608 | bytes 22021120 | tf_op jit(solution)/shard_map/dot_general | solution.py:50
  653.8 124.9 %all-reduce.12.cloned.1.call-done = f32[4096,256]{1,0:T(8,128)} async-done(((f32[4096,256]{1,0:T(8,128)}), f32[4096,256]{1,0:T(8,128)}) %all-reduce.12.cloned.1.call-update) | async-done | bytes 4194320 | tf_op jit(solution)/shard_map/psum | solution.py:44
  778.7 2.7 multiply_reduce_fusion
  781.5 6.6 psum.47
  788.1 33.5 %multiply_subtract_fusion = f32[1024,4096]{1,0:T(8,128)} fusion(f32[1024,4096]{1,0:T(8,128)} %convert_add_fusion, f32[4096,256]{1,0:T(8,128)} %all-reduce.12.cloned.1.call-done, f32[128,1024]{1,0:T(8,128)S(1)} %fusion.18, f32[128,1024]{1,0:T(8,128)S(1)} %fusion.11), kind=kOutput, calls=%fused_computation.7 | convolution fusion | flops 12893552640 | bytes 38797312 | tf_op jit(solution)/shard_map/dot_general | solution.py:47
  821.5 30.6 %multiply_convert_fusion = bf16[1024,4096]{1,0:T(8,128)(2,1)} fusion(f32[1024,4096]{1,0:T(8,128)} %fusion.5, f32[4096,256]{1,0:T(8,128)S(1)} %copy-done, f32[256]{0:T(256)S(1)} %add_rsqrt_fusion, f32[128,1024]{1,0:T(8,128)S(1)} %fusion.18, f32[128,1024]{1,0:T(8,128)S(1)} %fusion.11), kind=kOutput, calls=%fused_computation.6 | convolution fusion | flops 12898795520 | bytes 30409728 | tf_op jit(solution)/shard_map/dot_general | solution.py:50
  (59 shorter events, 20.7 us)
Async XLA Ops:
  7.2 59.5 %all-reduce.6.cloned.1.call-start = ((), (), s32[]{:S(2)}) async-start(), calls=%async_computation | async-start | bytes 2097152 | tf_op jit(solution)/shard_map/psum | solution.py:27
  27.5 93.0 %all-gather.5.cloned.1.call-start = ((), (), s32[]{:S(2)}) async-start(), calls=%async_computation.4 | async-start | bytes 2359296 | tf_op jit(solution)/shard_map/all_gather | solution.py:29
  70.8 303.9 %all-reduce.8.cloned.1.call-start = ((), (), s32[]{:S(2)}) async-start(), calls=%async_computation.1 | async-start | bytes 8388608 | tf_op jit(solution)/shard_map/psum | solution.py:44
  219.6 253.2 %all-reduce.10.cloned.1.call-start = ((), (), s32[]{:S(2)}) async-start(), calls=%async_computation.2 | async-start | bytes 2097152 | tf_op jit(solution)/shard_map/psum | solution.py:27
  437.8 88.8 %all-gather.7.cloned.1.call-start = ((), (), s32[]{:S(2)}) async-start(), calls=%async_computation.5 | async-start | bytes 2359296 | tf_op jit(solution)/shard_map/all_gather | solution.py:29
  476.9 301.8 %all-reduce.12.cloned.1.call-start = ((), (), s32[]{:S(2)}) async-start(), calls=%async_computation.3 | async-start | bytes 8388608 | tf_op jit(solution)/shard_map/psum | solution.py:44
  788.1 33.5 %copy-start = (f32[4096,256]{1,0:T(8,128)S(1)}, f32[4096,256]{1,0:T(8,128)}, u32[]{:S(2)}) copy-start(f32[4096,256]{1,0:T(8,128)} %all-reduce.12.cloned.1.call-done) | copy-start | bytes 12582916
Sparse Core Ops, SparseCore 0:
  27.7 39.0 all-reduce.5
  70.9 49.5 all-gather.4
  219.7 154.9 all-reduce.7
  438.0 34.7 all-reduce.9
  477.0 49.5 all-gather.6
  623.7 154.9 all-reduce.11
